TPU v7x, 256 devices: a whole 4x4x8 slice. The times are simulated.
256 devices in a mesh: strip: 64 (over z, x, core), frame: 4 (over y).
Axes of the slice: x: 4, y: 4, z: 8, core: 2. Of those that a mesh axis runs over, the one named last changes fastest.
Arguments:
- frames_in: bfloat16 [4, 256, 240, 768], P('frame', 'strip'), may hold values from -6 to 6
- dw_weight: float32 [7, 7, 768], replicated, may hold values from -0.875 to 0.875
- dw_bias: float32 [768], replicated, may hold values from -4 to 4
- ln_gain: float32 [768], replicated, may hold values from 0.5 to 2
- ln_bias: float32 [768], replicated, may hold values from -3 to 3
- w_in: bfloat16 [768, 3072], replicated, may hold values from -0.21875 to 0.21875
- b_in: float32 [3072], replicated, may hold values from -3 to 3
- w_out: bfloat16 [3072, 768], replicated, may hold values from -0.109375 to 0.109375
- b_out: float32 [768], replicated, may hold values from -3 to 3
- layer_scale: float32 [768], replicated, may hold values from 0.3 to 1.5
- depth_bins: int32 [4, 256, 240], P('frame', 'strip'), may hold values from -1 to 111, as said below
- return_counts: int32 [4, 256, 240], P('frame', 'strip'), may hold values from 1 to 4
Outputs:
- features: bfloat16 [4, 256, 240, 768], P('frame', 'strip')
- probe_stat: float32 [768, 112], replicated
Inputs may be any that keep to these rules, and one draw needn't show every extreme that they name: `depth_bins`: every row of every frame has at least one pixel with a return.
All inputs are finite; a program needn't handle non-finite values.
Results may differ from a plain program's by a relative error of at most 0.0056.
Values may be sent and summed in bfloat16 or wider, within the bound.
No kernel may reach another device: no remote copies, remote signals or barrier semaphores. Data moves between devices by JAX's collectives and lax.ppermute only.
A program may use at most 128 MiB of HBM per device.

v0:
```python
import jax
import jax.numpy as jnp
from jax import lax
from jax.sharding import PartitionSpec as P

BINS = 112
ridge = 0.05


def with_halo(cells, sides, width):
    for axis, dim in sides:
        count = lax.axis_size(axis)
        ends = count - 1
        head = lax.slice_in_dim(cells, 0, width, axis=dim)
        tail = lax.slice_in_dim(cells, cells.shape[dim] - width, cells.shape[dim], axis=dim)
        cells = jnp.concatenate(
            [
                lax.ppermute(tail, axis, [(i, (i + 1) % count) for i in range(ends)]),
                cells,
                lax.ppermute(head, axis, [((i + 1) % count, i) for i in range(ends)]),
            ],
            axis=dim,
        )
    return cells


def depthwise(padded, dw_weight, dw_bias, rows, cols):
    acc = jnp.zeros(padded.shape[:-3] + (rows, cols, padded.shape[-1]), jnp.float32) + dw_bias
    for a in range(7):
        for b in range(7):
            acc = (
                acc
                + padded[..., a : a + rows, b : b + cols, :].astype(jnp.float32) * dw_weight[a, b]
            )
    return acc


def block_tail(frame, conv, ln_gain, ln_bias, w_in, b_in, w_out, b_out, layer_scale):
    chans = frame.shape[-1]
    mean = jnp.mean(conv, axis=-1, keepdims=True)
    centered = conv - mean
    var = jnp.mean(centered * centered, axis=-1, keepdims=True)
    normed = (centered * lax.rsqrt(var + 1e-06) * ln_gain + ln_bias).astype(jnp.bfloat16)
    flat = normed.reshape(-1, chans)
    hidden = jax.nn.gelu(
        jnp.dot(flat, w_in, preferred_element_type=jnp.float32) + b_in, approximate=False
    ).astype(jnp.bfloat16)
    branch = jnp.dot(hidden, w_out, preferred_element_type=jnp.float32) + b_out
    merged = frame.reshape(-1, chans).astype(jnp.float32) + layer_scale * branch
    return merged.astype(jnp.bfloat16).reshape(frame.shape)


def cross_rows(left, right):
    return lax.dot_general(
        left, right, (((0,), (0,)), ((), ())), preferred_element_type=jnp.float32
    )


def per_device(
    frames_in,
    dw_weight,
    dw_bias,
    ln_gain,
    ln_bias,
    w_in,
    b_in,
    w_out,
    b_out,
    layer_scale,
    depth_bins,
    return_counts,
):
    rows = frames_in.shape[1]
    cols = frames_in.shape[2]
    chans = frames_in.shape[3]
    extended = with_halo(frames_in, (("strip", 1),), 3)
    extended = jnp.pad(extended, ((0, 0), (0, 0), (3, 3), (0, 0)))
    conv = depthwise(extended, dw_weight, dw_bias, rows, cols)
    features = block_tail(frames_in, conv, ln_gain, ln_bias, w_in, b_in, w_out, b_out, layer_scale)
    flat = features.reshape(-1, chans)
    bins_flat = depth_bins.reshape(-1)
    weight_int = jnp.where(bins_flat >= 0, return_counts.reshape(-1), 0)
    odd_weight = weight_int % 2
    even_weight = weight_int - odd_weight
    odd_rows = flat * odd_weight.astype(jnp.bfloat16)[:, None]
    even_rows = flat * even_weight.astype(jnp.bfloat16)[:, None]
    local_xx = cross_rows(odd_rows, flat) + cross_rows(even_rows, flat)
    matched = bins_flat[:, None] == jnp.arange(BINS, dtype=jnp.int32)[None, :]
    weighted_onehot = jnp.where(matched, weight_int[:, None], 0).astype(jnp.bfloat16)
    local_xy = cross_rows(flat, weighted_onehot)
    local_total = jnp.sum(weight_int.astype(jnp.float32))
    gram_xx, gram_xy, summed = lax.psum((local_xx, local_xy, local_total), ("strip", "frame"))
    system = gram_xx / summed + ridge * jnp.eye(chans, dtype=jnp.float32)
    lower = jnp.linalg.cholesky(system)
    probe = jax.scipy.linalg.cho_solve((lower, True), gram_xy / summed)
    return (features, probe * jnp.sqrt(summed * BINS))


def solution(mesh):
    placed = (
        P("frame", "strip", None, None),
        P(),
        P(),
        P(),
        P(),
        P(),
        P(),
        P(),
        P(),
        P(),
        P("frame", "strip", None),
        P("frame", "strip", None),
    )
    return jax.shard_map(
        per_device,
        mesh=mesh,
        in_specs=placed,
        out_specs=(P("frame", "strip", None, None), P()),
        check_vma=False,
    )
```

profile of v0, /device:TPU:99, one launch (start us, length us, event | category | flops | bytes accessed | tf_op | source)
XLA Modules:
  0.0 628.5 jit_solution(7905673559130028818)
XLA Ops:
  7.2 3.2 fusion.149
  10.4 3.7 collective-permute-start
  14.1 1.9 collective-permute-start.1
  16.7 10.1 %collective-permute-done = bf16[1,3,240,768]{3,2,1,0:T(8,128)(2,1)S(1)} collective-permute-done((bf16[1,3,240,768]{3,2,1,0:T(8,128)(2,1)}, bf16[1,3,240,768]{3,2,1,0:T(8,128)(2,1)S(1)}, u32[]{:S(2)}, u32[]{:S(2)}) %collective-permute-start) | collective-permute-done | bytes 1105952 | tf_op jit(solution)/shard_map/ppermute | solution.py:18
  27.1 4.1 collective-permute-done.1
  31.2 2.4 fusion.17
  33.5 1.3 constant_dynamic-update-slice_fusion.2
  34.9 22.8 %fusion.147 = (f32[4,240]{1,0:T(4,128)S(1)}, f32[1,4,240,768]{3,2,1,0:T(8,128)S(1)}) fusion(f32[768]{0:T(1024)S(1)} %get-tuple-element.61, bf16[1,10,246,768]{3,2,1,0:T(8,128)(2,1)S(1)} %fusion.17, f32[768]{0:T(1024)S(1)} %get-tuple-element.62, f32[768]{0:T(1024)S(1)} %get-tuple-element.15, f32[768]{0:T(1024)S(1)} %get-tuple-element.16, ...), kind=kLoop, calls=%fused_computation.295 | loop fusion | flops 109116480 | bytes 75360000 | tf_op jit(solution)/shard_map/reduce_sum | solution.py:40
  58.9 37.1 %fusion.20 = bf16[960,768]{1,0:T(8,128)(2,1)} fusion(bf16[3072,768]{1,0:T(8,128)(2,1)} %param.19, f32[3072]{0:T(1024)S(1)} %copy-done.11, bf16[960,768]{1,0:T(8,128)(2,1)S(1)} %bitcast.103, bf16[768,3072]{1,0:T(8,128)(2,1)} %param.17, f32[768]{0:T(1024)S(1)} %copy-done.12, f32[768]{0:T(1024)S(1)} %copy-done.13, bf16[1,4,240,768]{3,2,1,0:T(8,128)(2,1)S(1)} %copy-done), kind=kOutput, calls=%fused_computation.32 | convolution fusion | flops 9258024960 | bytes 13879296 | tf_op jit(solution)/shard_map/dot_general | solution.py:48
  96.1 2.9 fusion.45
  98.9 3.6 fusion.22
  102.5 3.0 fusion.28
  106.2 77.6 %psum.22 = f32[]{:T(128)} all-reduce(f32[]{:T(128)} %convert_reduce_fusion), channel_id=1, replica_groups=mesh['strip'=64,'frame'=4] {'strip','frame'}, use_global_device_ids=true, to_apply=%region_4.5 | all-reduce | flops 1 | bytes 8 | tf_op jit(solution)/shard_map/psum | solution.py:92
  184.5 191.4 %all-reduce.5.cloned.1.call-done = (f32[768,768]{0,1:T(8,128)}, f32[768,112]{0,1:T(8,128)}) async-done(((f32[768,768]{0,1:T(8,128)}, f32[768,112]{0,1:T(8,128)}), (f32[768,768]{0,1:T(8,128)}, f32[768,112]{0,1:T(8,128)})) %all-reduce.5.cloned.1.call-update) | async-done | bytes 2703376 | tf_op jit(solution)/shard_map/psum | solution.py:92
  375.9 3.9 select_add_fusion
  379.8 3.2 copy.16
  383.0 2.6 fusion.21
  385.6 1.4 copy-done.3
  387.0 11.7 %cholesky.164 = f32[128,128]{1,0:T(8,128)S(1)} custom-call(f32[128,128]{1,0:T(8,128)S(1)} %cholesky.421), custom_call_target="Cholesky" | custom-call | tf_op jit(solution)/shard_map/jit(cholesky)/cholesky | solution.py:94
  398.8 9.8 %custom-call.50 = f32[1,128,128]{1,2,0:T(8,128)S(1)} custom-call(f32[1,128,128]{2,1,0:T(8,128)S(1)} %get-tuple-element.92), custom_call_target="InvertDiagBlocksLowerTriangular" | custom-call | tf_op jit(solution)/shard_map/jit(cholesky)/cholesky | solution.py:94
  408.6 1.4 fusion.39
  410.0 1.4 convolution_subtract_fusion
  411.4 11.7 %cholesky.187 = f32[128,128]{1,0:T(8,128)S(1)} custom-call(f32[128,128]{1,0:T(8,128)S(1)} %cholesky.425), custom_call_target="Cholesky" | custom-call | tf_op jit(solution)/shard_map/jit(cholesky)/cholesky | solution.py:94
  423.5 9.9 %custom-call.51 = f32[1,128,128]{1,2,0:T(8,128)S(1)} custom-call(f32[1,128,128]{2,1,0:T(8,128)S(1)} %get-tuple-element.90), custom_call_target="InvertDiagBlocksLowerTriangular" | custom-call | tf_op jit(solution)/shard_map/jit(cholesky)/cholesky | solution.py:94
  434.1 1.9 convolution_subtract_fusion.1
  436.0 11.7 %cholesky.352 = f32[128,128]{1,0:T(8,128)S(1)} custom-call(f32[128,128]{1,0:T(8,128)S(1)} %cholesky.430), custom_call_target="Cholesky" | custom-call | tf_op jit(solution)/shard_map/jit(cholesky)/cholesky | solution.py:94
  447.9 9.8 %custom-call.52 = f32[1,128,128]{1,2,0:T(8,128)S(1)} custom-call(f32[1,128,128]{2,1,0:T(8,128)S(1)} %get-tuple-element.88), custom_call_target="InvertDiagBlocksLowerTriangular" | custom-call | tf_op jit(solution)/shard_map/jit(cholesky)/cholesky | solution.py:94
  458.1 2.1 convolution_subtract_fusion.2
  460.2 11.9 %cholesky.371 = f32[128,128]{1,0:T(8,128)S(1)} custom-call(f32[128,128]{1,0:T(8,128)S(1)} %cholesky.435), custom_call_target="Cholesky" | custom-call | tf_op jit(solution)/shard_map/jit(cholesky)/cholesky | solution.py:94
  472.3 9.8 %custom-call.53 = f32[1,128,128]{1,2,0:T(8,128)S(1)} custom-call(f32[1,128,128]{2,1,0:T(8,128)S(1)} %get-tuple-element.86), custom_call_target="InvertDiagBlocksLowerTriangular" | custom-call | tf_op jit(solution)/shard_map/jit(cholesky)/cholesky | solution.py:94
  482.4 1.9 convolution_subtract_fusion.3
  484.3 11.7 %cholesky.390 = f32[128,128]{1,0:T(8,128)S(1)} custom-call(f32[128,128]{1,0:T(8,128)S(1)} %cholesky.440), custom_call_target="Cholesky" | custom-call | tf_op jit(solution)/shard_map/jit(cholesky)/cholesky | solution.py:94
  496.2 9.8 %custom-call.54 = f32[1,128,128]{1,2,0:T(8,128)S(1)} custom-call(f32[1,128,128]{2,1,0:T(8,128)S(1)} %get-tuple-element.84), custom_call_target="InvertDiagBlocksLowerTriangular" | custom-call | tf_op jit(solution)/shard_map/jit(cholesky)/cholesky | solution.py:94
  506.3 1.8 convolution_subtract_fusion.4
  508.1 11.7 %cholesky.408 = f32[128,128]{1,0:T(8,128)S(1)} custom-call(f32[128,128]{1,0:T(8,128)S(1)} %convolution_subtract_fusion.4), custom_call_target="Cholesky" | custom-call | tf_op jit(solution)/shard_map/jit(cholesky)/cholesky | solution.py:94
  527.1 1.6 select_select_fusion
  528.7 21.1 %while.1 = (s32[]{:T(128)}, f32[768,768]{0,1:T(8,128)}, s32[6,2]{0,1:T(2,128)S(1)}, f32[6,128,128]{2,1,0:T(8,128)}, s32[]{:T(128)}) while((s32[]{:T(128)}, f32[768,768]{0,1:T(8,128)}, s32[6,2]{0,1:T(2,128)S(1)}, f32[6,128,128]{2,1,0:T(8,128)}, s32[]{:T(128)}) %tuple.86), condition=%wide.while_cond, body=%wide.while_body.sunk | while | flops 2 | bytes 393829 | solution.py:95
  529.3 2.2 dynamic-slice.7
  532.8 2.2 dynamic-slice.7
  536.3 2.2 dynamic-slice.7
  539.9 2.2 dynamic-slice.7
  543.4 2.2 dynamic-slice.7
  546.9 2.1 dynamic-slice.7
  549.8 59.9 %custom-call.55 = f32[6,128,128]{1,2,0:T(8,128)S(1)} custom-call(f32[6,128,128]{2,1,0:T(8,128)} %get-tuple-element.9), custom_call_target="InvertDiagBlocksLowerTriangular" | custom-call | tf_op jit(solution)/shard_map/jit(_cho_solve)/triangular_solve | solution.py:95
  610.6 1.0 convolution_subtract_fusion.8
  611.8 1.2 convolution_subtract_fusion.7
  613.2 1.3 convolution_subtract_fusion.12
  614.7 1.3 convolution_subtract_fusion.11
  (135 shorter events, 23.1 us)
Async XLA Ops:
  7.2 19.7 %copy-start = (bf16[1,4,240,768]{3,2,1,0:T(8,128)(2,1)S(1)}, bf16[1,4,240,768]{3,2,1,0:T(8,128)(2,1)}, u32[]{:S(2)}) copy-start(bf16[1,4,240,768]{3,2,1,0:T(8,128)(2,1)} %param.12) | copy-start | bytes 4423684
  7.2 8.9 %copy-start.7 = (s32[1,4,240]{2,1,0:T(4,128)S(1)}, s32[1,4,240]{2,1,0:T(4,128)}, u32[]{:S(2)}) copy-start(s32[1,4,240]{2,1,0:T(4,128)} %param.22) | copy-start | bytes 11524
  7.2 9.0 %copy-start.6 = (s32[1,4,240]{2,1,0:T(4,128)S(1)}, s32[1,4,240]{2,1,0:T(4,128)}, u32[]{:S(2)}) copy-start(s32[1,4,240]{2,1,0:T(4,128)} %param.23) | copy-start | bytes 11524
  7.2 9.0 %copy-start.5 = (f32[7,7,768]{2,1,0:T(8,128)S(1)}, f32[7,7,768]{2,1,0:T(8,128)}, u32[]{:S(2)}) copy-start(f32[7,7,768]{2,1,0:T(8,128)} %param.13) | copy-start | bytes 451588
  7.2 368.7 %all-reduce.5.cloned.1.call-start = ((), (), s32[]{:S(2)}) async-start(), calls=%async_computation | async-start | bytes 5406720 | tf_op jit(solution)/shard_map/psum | solution.py:92
  10.4 16.3 %collective-permute-start = (bf16[1,3,240,768]{3,2,1,0:T(8,128)(2,1)}, bf16[1,3,240,768]{3,2,1,0:T(8,128)(2,1)S(1)}, u32[]{:S(2)}, u32[]{:S(2)}) collective-permute-start(bf16[1,3,240,768]{3,2,1,0:T(8,128)(2,1)} %get-tuple-element.81), channel_id=1, source_target_pairs={{0,4},{4,8},{8,12},{12,16},{16,20},{20,24},{24,28},{28,32},{32,36}... | collective-permute-start | bytes 3317768 | tf_op jit(solution)/shard_map/ppermute | solution.py:18
  14.1 17.0 %collective-permute-start.1 = (bf16[1,3,240,768]{3,2,1,0:T(8,128)(2,1)}, bf16[1,3,240,768]{3,2,1,0:T(8,128)(2,1)}, u32[]{:S(2)}, u32[]{:S(2)}) collective-permute-start(bf16[1,3,240,768]{3,2,1,0:T(8,128)(2,1)} %get-tuple-element.82), channel_id=1, source_target_pairs={{4,0},{8,4},{12,8},{16,12},{20,16},{24,20},{28,24},{32,28},{36,32}... | collective-permute-start | bytes 3317768 | tf_op jit(solution)/shard_map/ppermute | solution.py:20
  27.1 7.8 %copy-start.8 = (f32[768]{0:T(1024)S(1)}, f32[768]{0:T(1024)}, u32[]{:S(2)}) copy-start(f32[768]{0:T(1024)} %param.14) | copy-start | bytes 9220
  57.7 0.7 copy-start.9
  57.7 0.7 copy-start.10
  58.2 0.7 copy-start.11
  58.2 0.7 copy-start.12
  58.2 0.7 copy-start.13
  98.9 3.6 copy-start.14
  379.8 3.2 copy-start.1
  385.6 1.4 copy-start.3
  527.1 82.6 %copy-start.4 = (f32[768,112]{0,1:T(8,128)S(1)}, f32[768,112]{0,1:T(8,128)}, u32[]{:S(2)}) copy-start(f32[768,112]{0,1:T(8,128)} %get-tuple-element.72) | copy-start | bytes 1032196
  549.8 66.4 %copy-start.2 = (f32[768,768]{0,1:T(8,128)S(1)}, f32[768,768]{0,1:T(8,128)}, u32[]{:S(2)}) copy-start(f32[768,768]{0,1:T(8,128)} %get-tuple-element.157) | copy-start | bytes 7077892
Sparse Core Ops, SparseCore 0:
  105.7 270.1 all-reduce.4
where the time goes:
time: 634 us; the launch traced here: 629 us
  other arithmetic  219 us (35%)
  waiting for transfers between devices  206 us (32%)
  blocking collectives  77.6 us (12%)
  matrix products  68.4 us (11%)
  local copies, waits for them, and re-layouts  32.2 us (5%)
  between operations  19.6 us (3%)
    psum x1, waiting for transfers between devices, per_device(): lax.psum((local_xx, local_xy, local_total), ('strip', 'frame'))  191 us
    another operation x22, other arithmetic, per_device(): lower = jnp.linalg.cholesky(system)  123 us
    psum x1, blocking collectives, per_device(): lax.psum((local_xx, local_xy, local_total), ('strip', 'frame'))  77.6 us
    another operation x3, other arithmetic, per_device(): probe = jax.scipy.linalg.cho_solve((lower, True), gram_xy / summed)  61.5 us
    dot_general x1, matrix products, block_tail(): branch = jnp.dot(hidden, w_out, preferred_element_type=jnp.float32) + b_out  37.1 us
    reduce_sum x1, other arithmetic, block_tail(): mean = jnp.mean(conv, axis=-1, keepdims=True)  22.8 us
    another operation x30, local copies, waits for them, and re-layouts  21 us
  transfers between devices with their start and end apart: 3, of which 3 were waited for; matrix products, arithmetic and copies ran while one was open for 0% of the time, Pallas kernels for 0%

commit v1 on v0

--- a/solution.py
+++ b/solution.py
@@ -2,6 +2,7 @@
 import jax.numpy as jnp
 from jax import lax
 from jax.sharding import PartitionSpec as P
+from jax.lax import psum
 
 BINS = 112
 ridge = 0.05
@@ -89,7 +90,13 @@
     weighted_onehot = jnp.where(matched, weight_int[:, None], 0).astype(jnp.bfloat16)
     local_xy = cross_rows(flat, weighted_onehot)
     local_total = jnp.sum(weight_int.astype(jnp.float32))
-    gram_xx, gram_xy, summed = lax.psum((local_xx, local_xy, local_total), ("strip", "frame"))
+
+    def _enter_field(original, link_axis, row_axis):
+        all_rows = psum(original, axis_name=link_axis)
+        vec_out = psum(all_rows, axis_name=row_axis)
+        return vec_out
+
+    gram_xx, gram_xy, summed = _enter_field((local_xx, local_xy, local_total), "strip", "frame")
     system = gram_xx / summed + ridge * jnp.eye(chans, dtype=jnp.float32)
     lower = jnp.linalg.cholesky(system)
     probe = jax.scipy.linalg.cho_solve((lower, True), gram_xy / summed)

time: 634 us -> 699 us (1.10)
  the two profiles are of different devices: /device:TPU:99 before, /device:TPU:0 now
where the time goes in v1:
time: 699 us; the launch traced here: 693 us
  other arithmetic  219 us (31%)
  waiting for transfers between devices  212 us (30%)
  blocking collectives  139 us (20%)
  matrix products  68.4 us (10%)
  local copies, waits for them, and re-layouts  32.1 us (5%)
  between operations  19.7 us (3%)
    psum x1, waiting for transfers between devices, _enter_field(): all_rows = psum(original, axis_name=link_axis)  209 us
    psum x1, blocking collectives, _enter_field(): all_rows = psum(original, axis_name=link_axis)  128 us
    another operation x22, other arithmetic, per_device(): lower = jnp.linalg.cholesky(system)  123 us
    another operation x3, other arithmetic, per_device(): probe = jax.scipy.linalg.cho_solve((lower, True), gram_xy / summed)  61.5 us
    dot_general x1, matrix products, block_tail(): branch = jnp.dot(hidden, w_out, preferred_element_type=jnp.float32) + b_out  37.1 us
    reduce_sum x1, other arithmetic, block_tail(): mean = jnp.mean(conv, axis=-1, keepdims=True)  22.8 us
    another operation x30, local copies, waits for them, and re-layouts  20.9 us
  transfers between devices with their start and end apart: 4, of which 3 were waited for; matrix products, arithmetic and copies ran while one was open for 0% of the time, Pallas kernels for 0%

profile of v1, /device:TPU:0, one launch (start us, length us, event | category | flops | bytes accessed | tf_op | source)
XLA Modules:
  0.0 693.4 jit_solution(15111667416066878239)
XLA Ops:
  7.2 3.2 fusion.149
  10.4 1.3 collective-permute-start
  11.8 1.3 collective-permute-start.1
  14.6 2.2 collective-permute-done.1
  16.8 2.4 fusion.17
  19.1 1.3 constant_dynamic-update-slice_fusion.2
  20.5 22.8 %fusion.147 = (f32[4,240]{1,0:T(4,128)S(1)}, f32[1,4,240,768]{3,2,1,0:T(8,128)S(1)}) fusion(f32[768]{0:T(1024)S(1)} %get-tuple-element.61, bf16[1,10,246,768]{3,2,1,0:T(8,128)(2,1)S(1)} %fusion.17, f32[768]{0:T(1024)S(1)} %get-tuple-element.62, f32[768]{0:T(1024)S(1)} %get-tuple-element.15, f32[768]{0:T(1024)S(1)} %get-tuple-element.16, ...), kind=kLoop, calls=%fused_computation.295 | loop fusion | flops 109116480 | bytes 75360000 | tf_op jit(solution)/shard_map/reduce_sum | solution.py:41
  44.5 37.1 %fusion.20 = bf16[960,768]{1,0:T(8,128)(2,1)} fusion(bf16[3072,768]{1,0:T(8,128)(2,1)} %param.19, f32[3072]{0:T(1024)S(1)} %copy-done.11, bf16[960,768]{1,0:T(8,128)(2,1)S(1)} %bitcast.103, bf16[768,3072]{1,0:T(8,128)(2,1)} %param.17, f32[768]{0:T(1024)S(1)} %copy-done.12, f32[768]{0:T(1024)S(1)} %copy-done.13, bf16[1,4,240,768]{3,2,1,0:T(8,128)(2,1)S(1)} %copy-done), kind=kOutput, calls=%fused_computation.32 | convolution fusion | flops 9258024960 | bytes 13879296 | tf_op jit(solution)/shard_map/dot_general | solution.py:49
  81.7 2.9 fusion.45
  84.6 3.6 fusion.22
  88.1 3.1 fusion.28
  91.3 209.0 %all-reduce.7.cloned.1.call-done = (f32[768,768]{0,1:T(8,128)}, f32[768,112]{0,1:T(8,128)}) async-done(((f32[768,768]{0,1:T(8,128)}, f32[768,112]{0,1:T(8,128)}), (f32[768,768]{0,1:T(8,128)}, f32[768,112]{0,1:T(8,128)})) %all-reduce.7.cloned.1.call-update) | async-done | bytes 2703376 | tf_op jit(solution)/shard_map/psum | solution.py:95
  300.9 128.2 %psum.44 = f32[]{:T(128)} all-reduce(f32[]{:T(128)} %convert_reduce_fusion), channel_id=1, replica_groups=mesh['strip'=64,'frame'=4] {'strip'}, use_global_device_ids=true, to_apply=%region_5.6 | all-reduce | flops 1 | bytes 8 | tf_op jit(solution)/shard_map/psum | solution.py:95
  429.0 11.1 %psum.45 = f32[]{:T(128)} all-reduce(f32[]{:T(128)} %psum.44), channel_id=1, replica_groups=mesh['strip'=64,'frame'=4] {'frame'}, use_global_device_ids=true, to_apply=%region_6.7 | all-reduce | flops 1 | bytes 8 | tf_op jit(solution)/shard_map/psum | solution.py:96
  440.9 3.9 select_add_fusion
  444.8 3.2 copy.16
  448.0 2.6 fusion.21
  450.6 1.4 copy-done.3
  452.0 11.7 %cholesky.164 = f32[128,128]{1,0:T(8,128)S(1)} custom-call(f32[128,128]{1,0:T(8,128)S(1)} %cholesky.421), custom_call_target="Cholesky" | custom-call | tf_op jit(solution)/shard_map/jit(cholesky)/cholesky | solution.py:101
  463.8 9.8 %custom-call.50 = f32[1,128,128]{1,2,0:T(8,128)S(1)} custom-call(f32[1,128,128]{2,1,0:T(8,128)S(1)} %get-tuple-element.94), custom_call_target="InvertDiagBlocksLowerTriangular" | custom-call | tf_op jit(solution)/shard_map/jit(cholesky)/cholesky | solution.py:101
  473.6 1.4 fusion.39
  475.0 1.4 convolution_subtract_fusion
  476.4 11.7 %cholesky.187 = f32[128,128]{1,0:T(8,128)S(1)} custom-call(f32[128,128]{1,0:T(8,128)S(1)} %cholesky.425), custom_call_target="Cholesky" | custom-call | tf_op jit(solution)/shard_map/jit(cholesky)/cholesky | solution.py:101
  488.5 9.9 %custom-call.51 = f32[1,128,128]{1,2,0:T(8,128)S(1)} custom-call(f32[1,128,128]{2,1,0:T(8,128)S(1)} %get-tuple-element.92), custom_call_target="InvertDiagBlocksLowerTriangular" | custom-call | tf_op jit(solution)/shard_map/jit(cholesky)/cholesky | solution.py:101
  499.1 1.9 convolution_subtract_fusion.1
  501.0 11.7 %cholesky.352 = f32[128,128]{1,0:T(8,128)S(1)} custom-call(f32[128,128]{1,0:T(8,128)S(1)} %cholesky.430), custom_call_target="Cholesky" | custom-call | tf_op jit(solution)/shard_map/jit(cholesky)/cholesky | solution.py:101
  512.9 9.8 %custom-call.52 = f32[1,128,128]{1,2,0:T(8,128)S(1)} custom-call(f32[1,128,128]{2,1,0:T(8,128)S(1)} %get-tuple-element.90), custom_call_target="InvertDiagBlocksLowerTriangular" | custom-call | tf_op jit(solution)/shard_map/jit(cholesky)/cholesky | solution.py:101
  523.1 2.1 convolution_subtract_fusion.2
  525.2 11.9 %cholesky.371 = f32[128,128]{1,0:T(8,128)S(1)} custom-call(f32[128,128]{1,0:T(8,128)S(1)} %cholesky.435), custom_call_target="Cholesky" | custom-call | tf_op jit(solution)/shard_map/jit(cholesky)/cholesky | solution.py:101
  537.3 9.8 %custom-call.53 = f32[1,128,128]{1,2,0:T(8,128)S(1)} custom-call(f32[1,128,128]{2,1,0:T(8,128)S(1)} %get-tuple-element.88), custom_call_target="InvertDiagBlocksLowerTriangular" | custom-call | tf_op jit(solution)/shard_map/jit(cholesky)/cholesky | solution.py:101
  547.4 1.9 convolution_subtract_fusion.3
  549.3 11.7 %cholesky.390 = f32[128,128]{1,0:T(8,128)S(1)} custom-call(f32[128,128]{1,0:T(8,128)S(1)} %cholesky.440), custom_call_target="Cholesky" | custom-call | tf_op jit(solution)/shard_map/jit(cholesky)/cholesky | solution.py:101
  561.2 9.8 %custom-call.54 = f32[1,128,128]{1,2,0:T(8,128)S(1)} custom-call(f32[1,128,128]{2,1,0:T(8,128)S(1)} %get-tuple-element.86), custom_call_target="InvertDiagBlocksLowerTriangular" | custom-call | tf_op jit(solution)/shard_map/jit(cholesky)/cholesky | solution.py:101
  571.3 1.8 convolution_subtract_fusion.4
  573.1 11.7 %cholesky.408 = f32[128,128]{1,0:T(8,128)S(1)} custom-call(f32[128,128]{1,0:T(8,128)S(1)} %convolution_subtract_fusion.4), custom_call_target="Cholesky" | custom-call | tf_op jit(solution)/shard_map/jit(cholesky)/cholesky | solution.py:101
  592.1 1.6 select_select_fusion
  593.7 21.0 %while.1 = (s32[]{:T(128)}, f32[768,768]{0,1:T(8,128)}, s32[6,2]{0,1:T(2,128)S(1)}, f32[6,128,128]{2,1,0:T(8,128)}, s32[]{:T(128)}) while((s32[]{:T(128)}, f32[768,768]{0,1:T(8,128)}, s32[6,2]{0,1:T(2,128)S(1)}, f32[6,128,128]{2,1,0:T(8,128)}, s32[]{:T(128)}) %tuple.86), condition=%wide.while_cond, body=%wide.while_body.sunk | while | flops 2 | bytes 393829 | solution.py:102
  594.3 2.2 dynamic-slice.7
  597.8 2.2 dynamic-slice.7
  601.3 2.2 dynamic-slice.7
  604.8 2.2 dynamic-slice.7
  608.3 2.2 dynamic-slice.7
  611.8 2.1 dynamic-slice.7
  614.6 59.9 %custom-call.55 = f32[6,128,128]{1,2,0:T(8,128)S(1)} custom-call(f32[6,128,128]{2,1,0:T(8,128)} %get-tuple-element.9), custom_call_target="InvertDiagBlocksLowerTriangular" | custom-call | tf_op jit(solution)/shard_map/jit(_cho_solve)/triangular_solve | solution.py:102
  675.5 1.0 convolution_subtract_fusion.8
  676.7 1.2 convolution_subtract_fusion.7
  678.1 1.2 convolution_subtract_fusion.12
  679.6 1.3 convolution_subtract_fusion.11
  (139 shorter events, 23.8 us)
Async XLA Ops:
  7.2 7.2 %copy-start = (bf16[1,4,240,768]{3,2,1,0:T(8,128)(2,1)S(1)}, bf16[1,4,240,768]{3,2,1,0:T(8,128)(2,1)}, u32[]{:S(2)}) copy-start(bf16[1,4,240,768]{3,2,1,0:T(8,128)(2,1)} %param.12) | copy-start | bytes 4423684
  7.2 5.9 copy-start.7
  7.2 6.0 copy-start.6
  7.2 6.1 copy-start.5
  7.2 293.1 %all-reduce.7.cloned.1.call-start = ((), (), s32[]{:S(2)}) async-start(), calls=%async_computation | async-start | bytes 5406720 | tf_op jit(solution)/shard_map/psum | solution.py:95
  10.4 3.8 collective-permute-start
  11.8 5.0 collective-permute-start.1
  14.6 5.9 copy-start.8
  43.3 0.7 copy-start.9
  43.3 0.7 copy-start.10
  43.8 0.7 copy-start.11
  43.8 0.7 copy-start.12
  43.8 0.7 copy-start.13
  84.6 3.6 copy-start.14
  91.2 349.6 %all-reduce.9.cloned.1.call-start = ((), (), s32[]{:S(2)}) async-start(), calls=%async_computation.1 | async-start | bytes 5406720 | tf_op jit(solution)/shard_map/psum | solution.py:96
  444.8 3.2 copy-start.1
  450.6 1.4 copy-start.3
  592.1 82.5 %copy-start.4 = (f32[768,112]{0,1:T(8,128)S(1)}, f32[768,112]{0,1:T(8,128)}, u32[]{:S(2)}) copy-start(f32[768,112]{0,1:T(8,128)} %get-tuple-element.74) | copy-start | bytes 1032196
  614.6 66.4 %copy-start.2 = (f32[768,768]{0,1:T(8,128)S(1)}, f32[768,768]{0,1:T(8,128)}, u32[]{:S(2)}) copy-start(f32[768,768]{0,1:T(8,128)} %get-tuple-element.163) | copy-start | bytes 7077892
Sparse Core Ops, SparseCore 0:
  91.4 208.8 all-reduce.6
  302.7 72.6 all-reduce.8
